TPU v7x, 128 devices: a whole 4x4x4 slice. The times are simulated.
128 devices in a mesh: slab: 8 (over y, x_hi), brick: 16 (over x_lo, z, core).
Axes of the slice: x: 4 (x_hi: 2, x_lo: 2; x = x_hi * 2 + x_lo), y: 4, z: 4, core: 2. Of those that a mesh axis runs over, the one named last changes fastest.
Arguments:
- k_coeffs: float32 [16, 32, 16, 128], P('slab', 'brick'), may hold values from -0.3 to 0.4
- v_basis: float32 [32768, 128], P(('slab', 'brick')), may hold values from -4 to 4
Outputs:
- basis_x: float32 [16, 32, 16, 128], P('slab', 'brick')
- coupling: float32 [128, 128], replicated
- basis_v: float32 [32768, 128], P(('slab', 'brick'))
All inputs are finite; a program needn't handle non-finite values.
Results may differ from a plain program's by a relative error of at most 0.0001.
Values sent between devices are 32-bit elements; how exact they have to be, the bound alone decides.
No kernel may reach another device: no remote copies, remote signals or barrier semaphores. Data moves between devices by JAX's collectives and lax.ppermute only.
A program may use at most 64 MiB of HBM per device.

v0:
```python
import math
import jax
import jax.numpy as jnp
from jax import lax
from jax.sharding import PartitionSpec as P

NVX = 32
CFL = 0.9
VMAX = 6.0
COLLIDE = 0.3
RHO_MIN = 0.25
TEMP_MIN = 0.25
PRECISE = lax.Precision.HIGHEST


def with_halo(array, sides, width):
    edges = {}
    for axis, dim in sides:
        peers, length = (lax.axis_size(axis), array.shape[dim])
        up = [(i, (i + 1) % peers) for i in range(peers)]
        last = lax.slice_in_dim(array, length - width, length, axis=dim)
        leading = lax.slice_in_dim(array, 0, width, axis=dim)
        edges[dim] = (
            lax.ppermute(last, axis, up),
            lax.ppermute(leading, axis, [(b, a) for a, b in up]),
        )
    done = []
    for _, dim in sides:
        low, high = edges[dim]
        around = [(width, width) if d in done else (0, 0) for d in range(array.ndim)]
        array = jnp.concatenate([jnp.pad(low, around), array, jnp.pad(high, around)], axis=dim)
        done.append(dim)
    return array


def over_pieces(array, axis):
    parts = lax.all_gather(array, axis)
    return parts.sum(axis=0)


def velocities(indices):
    spacing = 2.0 * VMAX / NVX
    first_index = indices // (NVX * NVX)
    second = indices // NVX % NVX
    third_index = indices % NVX
    coords = jnp.stack([first_index, second, third_index]).astype(jnp.float32)
    return -VMAX + (coords + 0.5) * spacing


def maxwell(cell_params, velocity):
    distance = (velocity[0][None, :] - cell_params[1][:, None]) ** 2
    distance = distance + (velocity[1][None, :] - cell_params[2][:, None]) ** 2
    distance = distance + (velocity[2][None, :] - cell_params[3][:, None]) ** 2
    amplitude = cell_params[0] * (2.0 * math.pi * cell_params[4]) ** (-1.5)
    return amplitude[:, None] * jnp.exp(distance * (-0.5 / cell_params[4])[:, None])


def cell_state(vectors, coeffs):
    moments = lax.dot_general(vectors, coeffs, (((1,), (1,)), ((), ())), precision=PRECISE)
    density = jnp.maximum(moments[0], RHO_MIN)
    drift_speed = moments[1:4] / density[None, :]
    temper = jnp.maximum(
        (moments[4] / density - jnp.sum(drift_speed * drift_speed, axis=0)) / 3.0, TEMP_MIN
    )
    return jnp.concatenate([density[None], drift_speed, temper[None]], axis=0)


def transport_flux(backward, forward, transport):
    flux = jnp.zeros_like(backward[0])
    for axis_id in range(3):
        flux = flux + jnp.dot(backward[axis_id], transport[axis_id], precision=PRECISE)
        flux = flux + jnp.dot(forward[axis_id], transport[3 + axis_id], precision=PRECISE)
    return flux


def products(left_side, backward, forward, maxwell_proj):
    pieces = [
        lax.dot_general(left_side, item, (((0,), (0,)), ((), ())), precision=PRECISE)
        for item in backward + forward + [maxwell_proj]
    ]
    return jnp.stack(pieces)


def coupling_step(coupling_hat, minus_side, plus_side, projected, transport, time_step):
    drift_sum = jnp.zeros_like(coupling_hat)
    for axis_id in range(3):
        drift_sum = drift_sum + jnp.dot(
            jnp.dot(minus_side[axis_id], coupling_hat, precision=PRECISE),
            transport[axis_id],
            precision=PRECISE,
        )
        drift_sum = drift_sum + jnp.dot(
            jnp.dot(plus_side[axis_id], coupling_hat, precision=PRECISE),
            transport[3 + axis_id],
            precision=PRECISE,
        )
    return coupling_hat + time_step * drift_sum - COLLIDE * (projected - coupling_hat)


def velocity_step(velocity_part, minus_side, plus_side, back_proj, positive, negative, time_step):
    drift_sum = jnp.zeros_like(velocity_part)
    for axis_id in range(3):
        drift_sum = drift_sum + positive[axis_id][:, None] * jnp.dot(
            velocity_part, minus_side[axis_id].T, precision=PRECISE
        )
        drift_sum = drift_sum + negative[axis_id][:, None] * jnp.dot(
            velocity_part, plus_side[axis_id].T, precision=PRECISE
        )
    return velocity_part - time_step * drift_sum + COLLIDE * (back_proj - velocity_part)


def slopes(padded, lengths):
    rank_size = padded.shape[3]
    centre = padded[1:-1, 1:-1]
    backward = [
        (centre - padded[:-2, 1:-1]) * lengths[0],
        (centre - padded[1:-1, :-2]) * lengths[1],
        (centre - jnp.roll(centre, 1, axis=2)) * lengths[2],
    ]
    forward = [
        (padded[2:, 1:-1] - centre) * lengths[0],
        (padded[1:-1, 2:] - centre) * lengths[1],
        (jnp.roll(centre, -1, axis=2) - centre) * lengths[2],
    ]
    return (
        [item.reshape(-1, rank_size) for item in backward],
        [item.reshape(-1, rank_size) for item in forward],
    )


def local(k_coeffs, v_basis):
    cells_x, cells_y, cells_z, rank_size = k_coeffs.shape
    cell_count = cells_x * cells_y * cells_z
    slab_count = lax.axis_size("slab")
    brick_count = lax.axis_size("brick")
    devices = slab_count * brick_count
    lengths = (cells_x * slab_count, cells_y * brick_count, cells_z)
    time_step = CFL / (VMAX * (lengths[0] + lengths[1] + lengths[2]))
    weight_x = 1.0 / (lengths[0] * lengths[1] * lengths[2])
    weight_v = (2.0 * VMAX / NVX) ** 3
    row_count = v_basis.shape[0]
    device = lax.axis_index("slab") * brick_count + lax.axis_index("brick")
    row_ids = device * row_count + jnp.arange(row_count, dtype=jnp.int32)
    velocity = velocities(row_ids)
    positive = jnp.maximum(velocity, 0.0)
    negative = jnp.minimum(velocity, 0.0)
    weights = jnp.stack(
        [
            jnp.ones_like(velocity[0]),
            velocity[0],
            velocity[1],
            velocity[2],
            jnp.sum(velocity * velocity, axis=0),
        ]
    )
    vectors = jnp.dot(weights, v_basis, precision=PRECISE) * weight_v
    transport = jnp.stack(
        [
            lax.dot_general(
                v_basis * (side[axis_id] * weight_v)[:, None],
                v_basis,
                (((0,), (0,)), ((), ())),
                precision=PRECISE,
            )
            for side in (positive, negative)
            for axis_id in range(3)
        ]
    )
    transport, vectors = lax.psum((transport, vectors), ("slab", "brick"))
    coeff_flat = k_coeffs.reshape(cell_count, rank_size)
    cell_params = cell_state(vectors, coeff_flat)
    params_all = lax.all_gather(cell_params, ("slab", "brick"), axis=1, tiled=True)
    row_total = cell_count * devices
    block_rows = math.gcd(row_total, 512)

    def one_block(turn_index):
        part_params = lax.dynamic_slice_in_dim(
            params_all, 0 + turn_index * block_rows, block_rows, 1
        )
        return jnp.dot(maxwell(part_params, velocity), v_basis, precision=PRECISE) * weight_v

    blocks = lax.map(one_block, jnp.arange(row_total // block_rows, dtype=jnp.int32))
    whole_term = lax.psum(blocks.reshape(row_total, rank_size), ("slab", "brick"))
    maxwell_proj = lax.dynamic_slice_in_dim(whole_term, device * cell_count, cell_count, 0)
    padded = with_halo(k_coeffs, (("slab", 0), ("brick", 1)), 1)
    backward, forward = slopes(padded, lengths)
    advanced = (
        coeff_flat
        - time_step * transport_flux(backward, forward, transport)
        + COLLIDE * (maxwell_proj - coeff_flat)
    )
    identity = jnp.eye(rank_size, dtype=jnp.float32)
    padded_new = with_halo(
        advanced.reshape(cells_x, cells_y, cells_z, rank_size), (("slab", 0), ("brick", 1)), 1
    )
    backward, forward = slopes(padded_new, lengths)
    local_sums = jnp.concatenate(
        [
            lax.dot_general(advanced, advanced, (((0,), (0,)), ((), ())), precision=PRECISE)[None],
            products(advanced, backward, forward, maxwell_proj),
        ],
        axis=0,
    )
    reduced_all = lax.psum(local_sums * weight_x, ("slab", "brick"))
    factor = jnp.linalg.cholesky(reduced_all[0])
    inverse = jax.scipy.linalg.solve_triangular(factor, identity, lower=True)
    basis_new = jnp.dot(advanced, inverse.T, precision=PRECISE)
    mapped = jnp.einsum("ab,kbc,dc->kad", inverse, reduced_all[1:7], inverse, precision=PRECISE)
    minus_side = mapped[0:3]
    plus_side = mapped[3:6]
    projected = jnp.dot(inverse, reduced_all[7], precision=PRECISE)
    coupling_mid = coupling_step(factor.T, minus_side, plus_side, projected, transport, time_step)
    rows_piece = lax.all_gather(basis_new, ("slab", "brick"), axis=0, tiled=True)
    piece_rows = rows_piece.shape[0]
    fold_block_rows = math.gcd(piece_rows, 512)

    def add_block(turn_index, accumulated):
        offset = turn_index * fold_block_rows
        part_params = lax.dynamic_slice_in_dim(params_all, offset, fold_block_rows, 1)
        basis_block = lax.dynamic_slice_in_dim(rows_piece, offset, fold_block_rows, 0)
        values = maxwell(part_params, velocity)
        return (
            accumulated
            + lax.dot_general(values, basis_block, (((0,), (0,)), ((), ())), precision=PRECISE)
            * weight_x
        )

    back_proj = lax.fori_loop(
        0, piece_rows // fold_block_rows, add_block, jnp.zeros((row_count, rank_size), jnp.float32)
    )
    velocity_part = jnp.dot(v_basis, coupling_mid.T, precision=PRECISE)
    velocity_new = velocity_step(
        velocity_part, minus_side, plus_side, back_proj, positive, negative, time_step
    )
    gram_v = (
        lax.dot_general(velocity_new, velocity_new, (((0,), (0,)), ((), ())), precision=PRECISE)
        * weight_v
    )
    gram_v = over_pieces(gram_v, ("slab", "brick"))
    coupling = jnp.linalg.cholesky(gram_v)
    inverse_v = jax.scipy.linalg.solve_triangular(coupling, identity, lower=True)
    vbasis_new = jnp.dot(velocity_new, inverse_v.T, precision=PRECISE)
    return (basis_new.reshape(cells_x, cells_y, cells_z, rank_size), coupling, vbasis_new)


def solution(mesh):
    placed = (P("slab", "brick", None, None), P(("slab", "brick"), None))
    return jax.shard_map(
        local,
        mesh=mesh,
        in_specs=placed,
        out_specs=(P("slab", "brick", None, None), P(), P(("slab", "brick"), None)),
        check_vma=False,
    )
```

profile of v0, /device:TPU:1, one launch (start us, length us, event | category | flops | bytes accessed | tf_op | source)
XLA Modules:
  0.0 735.6 jit_solution(13024606328633485945)
XLA Ops:
  8.4 68.7 %psum.29 = f32[5,128]{1,0:T(8,128)S(1)} all-reduce(f32[5,128]{1,0:T(8,128)S(1)} %convolution_multiply_fusion.9), channel_id=1, replica_groups=mesh['slab'=8,'brick'=16] {'slab','brick'}, use_global_device_ids=true, to_apply=%region_2.3 | all-reduce | flops 640 | bytes 5120 | tf_op jit(solution)/shard_map/psum | solution.py:169
  78.1 34.4 %all-gather.1 = f32[128,64,5]{1,2,0:T(8,128)S(1)} all-gather(f32[1,64,5]{1,2,0:T(8,128)S(1)} %maximum_bitcast_fusion), channel_id=1, replica_groups=mesh['slab'=8,'brick'=16] {'slab','brick'}, dimensions={0}, use_global_device_ids=true | all-gather | bytes 165120 | tf_op jit(solution)/shard_map/all_gather | solution.py:172
  112.7 60.6 %while.24 = (s32[]{:T(128)}, f32[16,512,128]{2,1,0:T(8,128)}, s32[16]{0:T(128)S(1)}, f32[5,8192]{1,0:T(8,128)S(1)}, f32[3,256]{1,0:T(4,128)S(1)}, /*index=5*/f32...) while((s32[]{:T(128)}, f32[16,512,128]{2,1,0:T(8,128)}, ...), condition=%wide.region_5.6_spmd, body=%wide.region_4.5_spmd.sunk | while | flops 202704400 | bytes 433923 | solution.py:182
  114.1 2.5 fusion.232
  117.9 2.4 fusion.232
  121.7 2.4 fusion.232
  125.5 2.4 fusion.232
  129.2 2.4 fusion.232
  133.0 2.4 fusion.232
  136.8 2.4 fusion.232
  140.6 2.4 fusion.232
  144.3 2.4 fusion.232
  148.1 2.4 fusion.232
  151.9 2.4 fusion.232
  155.7 2.4 fusion.232
  159.5 2.4 fusion.232
  163.2 2.4 fusion.232
  167.0 2.5 fusion.232
  170.8 2.4 fusion.232
  184.1 3.9 collective-permute-start.1
  191.7 143.5 %all-reduce.10.cloned.1.call-done = (f32[6,128,128]{2,1,0:T(8,128)}, f32[8192,128]{1,0:T(8,128)}) async-done(((f32[6,128,128]{2,1,0:T(8,128)}, f32[8192,128]{1,0:T(8,128)}), (f32[6,128,128]{2,1,0:T(8,128)}, f32[8192,128]{1,0:T(8,128)})) %all-reduce.10.cloned.1.call-update) | async-done | bytes 4587536 | tf_op jit(solution)/shard_map/psum | solution.py:169
  344.1 4.2 collective-permute-start.6
  349.2 2.3 collective-permute-done.7
  355.3 144.6 %all-reduce.8.cloned.1.call-done = f32[8,128,128]{1,2,0:T(8,128)} async-done(((f32[8,128,128]{1,2,0:T(8,128)}), f32[8,128,128]{1,2,0:T(8,128)}) %all-reduce.8.cloned.1.call-update) | async-done | bytes 524304 | tf_op jit(solution)/shard_map/psum | solution.py:204
  501.6 11.7 %cholesky.44 = f32[128,128]{1,0:T(8,128)S(1)} custom-call(f32[128,128]{1,0:T(8,128)S(1)} %fusion.83), custom_call_target="Cholesky" | custom-call | tf_op jit(solution)/shard_map/jit(cholesky)/cholesky | solution.py:205
  514.7 9.8 %custom-call.7 = f32[1,128,128]{1,2,0:T(8,128)S(1)} custom-call(f32[1,128,128]{2,1,0:T(8,128)S(1)} %select_bitcast_fusion.1), custom_call_target="InvertDiagBlocksLowerTriangular" | custom-call | tf_op jit(solution)/shard_map/jit(_solve_triangular)/triangular_solve | solution.py:206
  539.1 52.7 %all-gather.5.cloned.1.call-done = f32[8192,128]{1,0:T(8,128)} async-done(((f32[64,128]{1,0:T(8,128)}), f32[8192,128]{1,0:T(8,128)}) %all-gather.5.cloned.1.call-update) | async-done | bytes 4194320 | tf_op jit(solution)/shard_map/all_gather | solution.py:213
  591.8 39.5 %while.25 = (s32[]{:T(128)}, f32[256,128]{1,0:T(8,128)S(1)}, f32[5,8192]{1,0:T(8,128)S(1)}, f32[3,256]{1,0:T(4,128)S(1)}, f32[8192,128]{1,0:T(8,128)}, /*index=5...) while((s32[]{:T(128)}, f32[256,128]{1,0:T(8,128)S(1)}, ...), condition=%wide.region_11.14_spmd.clone, body=%wide.region_10.13_spmd.clone.sunk | while | flops 202737168 | bytes 564477 | solution.py:228
  591.9 2.3 fusion.236
  594.4 2.3 fusion.236
  596.8 2.3 fusion.236
  599.3 2.3 fusion.236
  601.8 2.3 fusion.236
  604.2 2.3 fusion.236
  606.7 2.3 fusion.236
  609.2 2.3 fusion.236
  611.7 2.3 fusion.236
  614.1 2.3 fusion.236
  616.6 2.3 fusion.236
  619.1 2.3 fusion.236
  621.5 2.3 fusion.236
  624.0 2.3 fusion.236
  626.5 2.3 fusion.236
  628.9 2.3 fusion.236
  632.6 67.7 %all-gather.7.cloned.1.call-done = f32[16384,128]{1,0:T(8,128)} async-done(((f32[128,128]{1,0:T(8,128)}), f32[16384,128]{1,0:T(8,128)}) %all-gather.7.cloned.1.call-update) | async-done | bytes 8388624 | tf_op jit(solution)/shard_map/all_gather | solution.py:37
  700.3 3.8 reduce_sum.32
  704.3 11.7 %cholesky.55 = f32[128,128]{1,0:T(8,128)S(1)} custom-call(f32[128,128]{1,0:T(8,128)S(1)} %fusion.85), custom_call_target="Cholesky" | custom-call | tf_op jit(solution)/shard_map/jit(cholesky)/cholesky | solution.py:240
  717.9 9.8 %custom-call.8 = f32[1,128,128]{1,2,0:T(8,128)S(1)} custom-call(f32[1,128,128]{2,1,0:T(8,128)S(1)} %get-tuple-element.175), custom_call_target="InvertDiagBlocksLowerTriangular" | custom-call | tf_op jit(solution)/shard_map/jit(_solve_triangular)/triangular_solve | solution.py:241
  (208 shorter events, 65.0 us)
Async XLA Ops:
  7.2 328.0 %all-reduce.10.cloned.1.call-start = ((), (), s32[]{:S(2)}) async-start(), calls=%async_computation.3 | async-start | bytes 9175040 | tf_op jit(solution)/shard_map/psum | solution.py:169
  173.3 9.6 %copy-start.1 = (f32[2,2,16,128]{3,2,1,0:T(8,128)S(1)}, f32[2,2,16,128]{3,2,1,0:T(8,128)}, u32[]{:S(2)}) copy-start(f32[2,2,16,128]{3,2,1,0:T(8,128)} %param.9) | copy-start | bytes 98308
  182.0 0.8 copy-start.3
  182.8 317.0 %all-reduce.8.cloned.1.call-start = ((), (), s32[]{:S(2)}) async-start(), calls=%async_computation | async-start | bytes 1048576 | tf_op jit(solution)/shard_map/psum | solution.py:204
  182.9 6.3 collective-permute-start
  184.1 5.0 collective-permute-start.1
  188.0 1.4 collective-permute-start.2
  188.0 3.6 collective-permute-start.3
  335.1 198.1 %copy-start.2 = (f32[6,128,128]{2,1,0:T(8,128)S(1)}, f32[6,128,128]{2,1,0:T(8,128)}, u32[]{:S(2)}) copy-start(f32[6,128,128]{2,1,0:T(8,128)} %get-tuple-element.173) | copy-start | bytes 1179652
  341.5 7.2 collective-permute-start.4
  343.1 5.5 collective-permute-start.5
  344.1 5.0 collective-permute-start.6
  348.3 3.2 collective-permute-start.7
  351.5 185.9 %copy-start = (f32[256,128]{1,0:T(8,128)S(1)}, f32[256,128]{1,0:T(8,128)}, u32[]{:S(2)}) copy-start(f32[256,128]{1,0:T(8,128)} %get-tuple-element.425) | copy-start | bytes 393220
  355.2 236.6 %all-gather.5.cloned.1.call-start = ((), (), s32[]{:S(2)}) async-start(), calls=%async_computation.1 | async-start | bytes 4227072 | tf_op jit(solution)/shard_map/all_gather | solution.py:213
  525.7 174.7 %all-gather.7.cloned.1.call-start = ((), (), s32[]{:S(2)}) async-start(), calls=%async_computation.2 | async-start | bytes 8454144 | tf_op jit(solution)/shard_map/all_gather | solution.py:37
Sparse Core Ops, SparseCore 0:
  182.9 152.1 all-reduce.9
  355.3 144.4 all-reduce.7
  525.8 65.9 all-gather.4
  632.7 67.5 all-gather.6
where the time goes:
time: 738 us; the launch traced here: 736 us
  waiting for transfers between devices  414 us (56%)
  matrix products  113 us (15%)
  blocking collectives  103 us (14%)
  other arithmetic  55 us (7%)
  between operations  14.3 us (2%)
  starting transfers between devices  12.9 us (2%)
  local copies, waits for them, and re-layouts  11.6 us (2%)
  loops' own time  11.5 us (2%)
    psum x1, waiting for transfers between devices, local(): reduced_all = lax.psum(local_sums * weight_x, ('slab', 'brick'))  145 us
    psum x1, waiting for transfers between devices, local(): transport, vectors = lax.psum((transport, vectors), ('slab', 'brick'))  143 us
    psum x1, blocking collectives, local(): transport, vectors = lax.psum((transport, vectors), ('slab', 'brick'))  68.7 us
    all_gather x1, waiting for transfers between devices, over_pieces(): parts = lax.all_gather(array, axis)  67.7 us
    all_gather x1, waiting for transfers between devices, local(): lax.all_gather(basis_new, ('slab', 'brick'), axis=0, tiled=True)  52.7 us
    dot_general x16, matrix products, one_block(): jnp.dot(maxwell(part_params, velocity), v_basis, precision=PRECISE)  38.9 us
    dot_general x16, matrix products, add_block(): lax.dot_general(values, basis_block, (((0,), (0,)), ((), ())), precision=...  37.2 us
    all_gather x1, blocking collectives, local(): lax.all_gather(cell_params, ('slab', 'brick'), axis=1, tiled=True)  34.4 us
  transfers between devices with their start and end apart: 12, of which 9 were waited for; matrix products, arithmetic and copies ran while one was open for 2% of the time, Pallas kernels for 0%

commit v1 on v0

--- a/solution.py
+++ b/solution.py
@@ -169,7 +169,12 @@
     transport, vectors = lax.psum((transport, vectors), ("slab", "brick"))
     coeff_flat = k_coeffs.reshape(cell_count, rank_size)
     cell_params = cell_state(vectors, coeff_flat)
-    params_all = lax.all_gather(cell_params, ("slab", "brick"), axis=1, tiled=True)
+    params_all = jnp.concatenate(
+        lax.all_to_all(
+            jnp.stack([cell_params] * lax.axis_size(("slab", "brick"))), ("slab", "brick"), 0, 0
+        ),
+        axis=1,
+    )
     row_total = cell_count * devices
     block_rows = math.gcd(row_total, 512)
 

time: 738 us -> 700 us (0.949)
  blocking collectives: 103 us -> 68.7 us
  matrix products: 113 us -> 98.5 us
    all_gather x1 -> x0, blocking collectives: 34.4 us -> none  [local(): lax.all_gather(cell_params, ('slab', 'brick'), axis=1, tiled=True)]
    dot_general x16, matrix products: 38.9 us -> 24.4 us  [one_block(): jnp.dot(maxwell(part_params, velocity), v_basis, precision=PRECISE)]
  transfers between devices with their start and end apart: 12 -> 13, of which waited for: 9 -> 9; matrix products, arithmetic and copies ran while one was open for 2% -> 3% of each run, Pallas kernels for 0% -> 0%
where the time goes in v1:
time: 700 us; the launch traced here: 698 us
  waiting for transfers between devices  418 us (60%)
  matrix products  98.5 us (14%)
  blocking collectives  68.7 us (10%)
  other arithmetic  56.2 us (8%)
  starting transfers between devices  18.5 us (3%)
  between operations  14.4 us (2%)
  local copies, waits for them, and re-layouts  13.2 us (2%)
  loops' own time  11.5 us (2%)
    psum x1, waiting for transfers between devices, local(): transport, vectors = lax.psum((transport, vectors), ('slab', 'brick'))  145 us
    psum x1, waiting for transfers between devices, local(): reduced_all = lax.psum(local_sums * weight_x, ('slab', 'brick'))  144 us
    psum x1, blocking collectives, local(): transport, vectors = lax.psum((transport, vectors), ('slab', 'brick'))  68.7 us
    all_gather x1, waiting for transfers between devices, over_pieces(): parts = lax.all_gather(array, axis)  67.7 us
    all_gather x1, waiting for transfers between devices, local(): lax.all_gather(basis_new, ('slab', 'brick'), axis=0, tiled=True)  52.7 us
    dot_general x16, matrix products, add_block(): lax.dot_general(values, basis_block, (((0,), (0,)), ((), ())), precision=...  37.2 us
    dot_general x16, matrix products, one_block(): jnp.dot(maxwell(part_params, velocity), v_basis, precision=PRECISE)  24.4 us
  transfers between devices with their start and end apart: 13, of which 9 were waited for; matrix products, arithmetic and copies ran while one was open for 3% of the time, Pallas kernels for 0%

profile of v1, /device:TPU:1, one launch (start us, length us, event | category | flops | bytes accessed | tf_op | source)
XLA Modules:
  0.0 698.5 jit_solution(17623881068459565311)
XLA Ops:
  8.4 68.7 %psum.29 = f32[5,128]{1,0:T(8,128)S(1)} all-reduce(f32[5,128]{1,0:T(8,128)S(1)} %convolution_multiply_fusion.9), channel_id=1, replica_groups=mesh['slab'=8,'brick'=16] {'slab','brick'}, use_global_device_ids=true, to_apply=%region_2.3 | all-reduce | flops 640 | bytes 5120 | tf_op jit(solution)/shard_map/psum | solution.py:169
  79.1 4.7 all-to-all-start
  92.6 1.5 all-to-all-done
  96.1 46.1 %while.24 = (s32[]{:T(128)}, f32[16,512,128]{2,1,0:T(8,128)}, s32[16]{0:T(128)S(1)}, f32[5,8192]{1,0:T(8,128)S(1)}, f32[3,256]{1,0:T(4,128)S(1)}, /*index=5*/f32...) while((s32[]{:T(128)}, f32[16,512,128]{2,1,0:T(8,128)}, ...), condition=%wide.region_5.6_spmd, body=%wide.region_4.5_spmd.sunk | while | flops 202704400 | bytes 433923 | solution.py:187
  97.5 1.5 fusion.232
  100.3 1.5 fusion.232
  103.2 1.5 fusion.232
  108.9 1.5 fusion.232
  111.8 1.5 fusion.232
  117.6 1.5 fusion.232
  120.5 1.5 fusion.232
  123.3 1.5 fusion.232
  126.2 1.5 fusion.232
  134.8 1.5 fusion.232
  137.7 1.6 fusion.232
  140.6 1.5 fusion.232
  144.3 3.7 collective-permute-start.1
  150.3 2.3 collective-permute-done.3
  152.7 145.3 %all-reduce.10.cloned.1.call-done = (f32[6,128,128]{2,1,0:T(8,128)}, f32[8192,128]{1,0:T(8,128)}) async-done(((f32[6,128,128]{2,1,0:T(8,128)}, f32[8192,128]{1,0:T(8,128)}), (f32[6,128,128]{2,1,0:T(8,128)}, f32[8192,128]{1,0:T(8,128)})) %all-reduce.10.cloned.1.call-update) | async-done | bytes 4587536 | tf_op jit(solution)/shard_map/psum | solution.py:169
  304.3 1.6 collective-permute-start.4
  306.9 4.2 collective-permute-start.6
  312.0 2.3 collective-permute-done.7
  318.2 144.4 %all-reduce.8.cloned.1.call-done = f32[8,128,128]{1,2,0:T(8,128)} async-done(((f32[8,128,128]{1,2,0:T(8,128)}), f32[8,128,128]{1,2,0:T(8,128)}) %all-reduce.8.cloned.1.call-update) | async-done | bytes 524304 | tf_op jit(solution)/shard_map/psum | solution.py:209
  464.4 11.7 %cholesky.44 = f32[128,128]{1,0:T(8,128)S(1)} custom-call(f32[128,128]{1,0:T(8,128)S(1)} %fusion.83), custom_call_target="Cholesky" | custom-call | tf_op jit(solution)/shard_map/jit(cholesky)/cholesky | solution.py:210
  477.5 9.8 %custom-call.7 = f32[1,128,128]{1,2,0:T(8,128)S(1)} custom-call(f32[1,128,128]{2,1,0:T(8,128)S(1)} %select_bitcast_fusion.1), custom_call_target="InvertDiagBlocksLowerTriangular" | custom-call | tf_op jit(solution)/shard_map/jit(_solve_triangular)/triangular_solve | solution.py:211
  498.5 1.8 fusion.52
  501.9 52.7 %all-gather.4.cloned.1.call-done = f32[8192,128]{1,0:T(8,128)} async-done(((f32[64,128]{1,0:T(8,128)}), f32[8192,128]{1,0:T(8,128)}) %all-gather.4.cloned.1.call-update) | async-done | bytes 4194320 | tf_op jit(solution)/shard_map/all_gather | solution.py:218
  554.6 39.5 %while.25 = (s32[]{:T(128)}, f32[256,128]{1,0:T(8,128)S(1)}, f32[5,8192]{1,0:T(8,128)S(1)}, f32[3,256]{1,0:T(4,128)S(1)}, f32[8192,128]{1,0:T(8,128)}, /*index=5...) while((s32[]{:T(128)}, f32[256,128]{1,0:T(8,128)S(1)}, ...), condition=%wide.region_11.14_spmd.clone, body=%wide.region_10.13_spmd.clone.sunk | while | flops 202737168 | bytes 564477 | solution.py:233
  554.7 2.3 fusion.236
  557.2 2.3 fusion.236
  559.6 2.3 fusion.236
  562.1 2.3 fusion.236
  564.6 2.3 fusion.236
  567.1 2.3 fusion.236
  569.5 2.3 fusion.236
  572.0 2.3 fusion.236
  574.5 2.3 fusion.236
  576.9 2.3 fusion.236
  579.4 2.3 fusion.236
  581.9 2.3 fusion.236
  584.3 2.3 fusion.236
  586.8 2.3 fusion.236
  589.3 2.3 fusion.236
  591.7 2.3 fusion.236
  595.4 67.7 %all-gather.6.cloned.1.call-done = f32[16384,128]{1,0:T(8,128)} async-done(((f32[128,128]{1,0:T(8,128)}), f32[16384,128]{1,0:T(8,128)}) %all-gather.6.cloned.1.call-update) | async-done | bytes 8388624 | tf_op jit(solution)/shard_map/all_gather | solution.py:37
  663.2 3.8 reduce_sum.32
  667.1 11.7 %cholesky.55 = f32[128,128]{1,0:T(8,128)S(1)} custom-call(f32[128,128]{1,0:T(8,128)S(1)} %fusion.85), custom_call_target="Cholesky" | custom-call | tf_op jit(solution)/shard_map/jit(cholesky)/cholesky | solution.py:245
  680.8 9.8 %custom-call.8 = f32[1,128,128]{1,2,0:T(8,128)S(1)} custom-call(f32[1,128,128]{2,1,0:T(8,128)S(1)} %get-tuple-element.175), custom_call_target="InvertDiagBlocksLowerTriangular" | custom-call | tf_op jit(solution)/shard_map/jit(_solve_triangular)/triangular_solve | solution.py:246
  (214 shorter events, 69.3 us)
Async XLA Ops:
  7.2 88.9 %copy-start = (f32[256,128]{1,0:T(8,128)S(1)}, f32[256,128]{1,0:T(8,128)}, u32[]{:S(2)}) copy-start(f32[256,128]{1,0:T(8,128)} %param.10) | copy-start | bytes 393220
  79.1 15.0 %all-to-all-start = ((f32[128,1,320]{2,1,0:T(1,128)}), f32[128,1,320]{2,1,0:T(1,128)S(1)}, u32[]{:S(2)}, u32[]{:S(2)}) async-start(f32[128,1,320]{2,1,0:T(1,128)} %reshape.322), calls=%async_computation | async-start | bytes 393216 | tf_op jit(solution)/shard_map/all_to_all | solution.py:173
  83.8 214.2 %all-reduce.10.cloned.1.call-start = ((), (), s32[]{:S(2)}) async-start(), calls=%async_computation.4 | async-start | bytes 9175040 | tf_op jit(solution)/shard_map/psum | solution.py:169
  92.6 3.5 copy-start.3
  142.1 0.8 copy-start.1
  142.2 320.5 %all-reduce.8.cloned.1.call-start = ((), (), s32[]{:S(2)}) async-start(), calls=%async_computation.1 | async-start | bytes 1048576 | tf_op jit(solution)/shard_map/psum | solution.py:209
  142.9 6.6 collective-permute-start
  144.3 5.2 collective-permute-start.1
  148.0 2.3 collective-permute-start.2
  149.5 3.2 collective-permute-start.3
  297.9 198.1 %copy-start.2 = (f32[6,128,128]{2,1,0:T(8,128)S(1)}, f32[6,128,128]{2,1,0:T(8,128)}, u32[]{:S(2)}) copy-start(f32[6,128,128]{2,1,0:T(8,128)} %get-tuple-element.173) | copy-start | bytes 1179652
  304.3 7.2 %collective-permute-start.4 = (f32[1,2,16,128]{3,2,1,0:T(8,128)S(1)}, f32[1,2,16,128]{3,2,1,0:T(8,128)S(1)}, u32[]{:S(2)}, u32[]{:S(2)}) collective-permute-start(f32[1,2,16,128]{3,2,1,0:T(8,128)S(1)} %bitcast.335), channel_id=1, source_target_pairs={{0,16},{16,32},{32,48},{48,64},{64,80},{80,96},{96,112},{112,0},{1... | collective-permute-start | bytes 49160 | tf_op jit(solution)/shard_map/ppermute | solution.py:24
  305.9 5.5 collective-permute-start.5
  306.9 5.0 collective-permute-start.6
  311.1 3.2 collective-permute-start.7
  318.0 236.6 %all-gather.4.cloned.1.call-start = ((), (), s32[]{:S(2)}) async-start(), calls=%async_computation.2 | async-start | bytes 4227072 | tf_op jit(solution)/shard_map/all_gather | solution.py:218
  488.5 174.7 %all-gather.6.cloned.1.call-start = ((), (), s32[]{:S(2)}) async-start(), calls=%async_computation.3 | async-start | bytes 8454144 | tf_op jit(solution)/shard_map/all_gather | solution.py:37
Sparse Core Ops, SparseCore 0:
  142.3 155.6 all-reduce.9
  318.1 144.4 all-reduce.7
  488.6 65.9 all-gather.3
  595.6 67.5 all-gather.5
